TPU v7x, 32 devices: a whole 2x2x4 slice. The times are simulated.
32 devices in a mesh: had: 4 (over z), blk: 8 (over y, x, core).
Axes of the slice: x: 2, y: 2, z: 4, core: 2. Of those that a mesh axis runs over, the one named last changes fastest.
Arguments:
- panel: bfloat16 [65536, 512], P(('had', 'blk')), may hold values from -100 to 100
- signs: int32 [65536], P(('had', 'blk')), may hold values from 0 to 1
- sample_rows: int32 [8, 2048], P('blk'), may hold values from 0 to 8191
Outputs:
- q_panel: bfloat16 [65536, 512], P(('had', 'blk'))
- r_sketch: float32 [512, 512], replicated
- r_gram: float32 [512, 512], replicated
All inputs are finite; a program needn't handle non-finite values.
Results may differ from a plain program's by a relative error of at most 0.0075.
The roundings to bfloat16 on the way count: a program that leaves them out, or rounds other values in their place, can miss the bound.
Values sent between devices are 32-bit elements; how exact they have to be, the bound alone decides.
A program may use at most 448 MiB of HBM per device.

v0:
```python
import math
import jax
import jax.numpy as jnp
from jax import lax
from jax.sharding import PartitionSpec as P

LH = 32


def bit_parity(value):
    counted = jnp.zeros_like(value)
    for shift_count in range(16):
        counted = counted + jnp.bitwise_and(jnp.right_shift(value, shift_count), 1)
    return counted % 2


def hadamard(order):
    first = lax.broadcasted_iota(jnp.int32, (order, order), 0)
    second = lax.broadcasted_iota(jnp.int32, (order, order), 1)
    parity = bit_parity(jnp.bitwise_and(first, second))
    return (1 - 2 * parity).astype(jnp.float32)


def upper_factor(matrix):
    return jnp.linalg.cholesky(matrix).T


def lower_inverse(lower):
    order = lower.shape[0]
    inverse = (1.0 / jnp.diagonal(lower)).reshape(order, 1, 1)
    width = 1
    while width < order:
        count = order // (2 * width)
        tiles = lower.reshape(count, 2 * width, count, 2 * width)
        diag_tiles = jnp.moveaxis(jnp.diagonal(tiles, axis1=0, axis2=2), -1, 0)
        corner = diag_tiles[:, width:, :width]
        first_inv = inverse[0::2]
        second_inv = inverse[1::2]
        partial_value = jnp.einsum(
            "ajk,akl->ajl", corner, first_inv, precision=lax.Precision.HIGHEST
        )
        lower_left = -jnp.einsum(
            "aij,ajl->ail", second_inv, partial_value, precision=lax.Precision.HIGHEST
        )
        zero_tile = jnp.zeros_like(corner)
        top_half = jnp.concatenate([first_inv, zero_tile], axis=2)
        bottom_half = jnp.concatenate([lower_left, second_inv], axis=2)
        inverse = jnp.concatenate([top_half, bottom_half], axis=1)
        width = width * 2
    return inverse[0]


def inverse_upper(factor):
    return lower_inverse(factor.T).T


def on_device(panel, signs, sample_rows):
    n_had = lax.axis_size("had")
    n_blk = lax.axis_size("blk")
    my_group = lax.axis_index("had")
    rows_dev, columns = panel.shape
    sketch_count = sample_rows.shape[1]
    groups = rows_dev // LH
    flipped = jnp.where(signs[:, None] == 1, -panel, panel)
    inner = hadamard(LH).astype(jnp.bfloat16)
    mixed = jnp.einsum(
        "ml,glk->gmk",
        inner,
        flipped.reshape(groups, LH, columns),
        preferred_element_type=jnp.float32,
    )
    mixed = mixed.reshape(rows_dev, columns)
    picks = sample_rows[0]
    owners = picks // rows_dev
    offsets = picks % rows_dev
    factor = 1.0 / math.sqrt(n_had * LH * sketch_count * n_blk)
    parity = bit_parity(jnp.bitwise_and(owners, my_group))
    weights = (1 - 2 * parity).astype(jnp.float32) * factor
    partial_sketch = jnp.take(mixed, offsets, axis=0) * weights[:, None]
    sketch = lax.psum(partial_sketch, ("had", "blk"))
    sketch_gram = jnp.dot(
        sketch.T, sketch, precision=lax.Precision.HIGHEST, preferred_element_type=jnp.float32
    )
    r_sketch = upper_factor(sketch_gram)
    sketch_inverse = inverse_upper(r_sketch).astype(jnp.bfloat16)
    whitened = jnp.dot(panel, sketch_inverse, preferred_element_type=jnp.float32).astype(
        jnp.bfloat16
    )
    partial_gram = jnp.einsum("rk,rj->kj", whitened, whitened, preferred_element_type=jnp.float32)
    summed = lax.psum(partial_gram, ("had", "blk"))
    gram_matrix = summed / (rows_dev * n_had * n_blk)
    r_gram = upper_factor(gram_matrix)
    gram_inverse = inverse_upper(r_gram).astype(jnp.bfloat16)
    q_panel = jnp.dot(whitened, gram_inverse, preferred_element_type=jnp.float32).astype(
        jnp.bfloat16
    )
    return (q_panel, r_sketch, r_gram)


def solution(mesh):
    placed = (P(("had", "blk"), None), P(("had", "blk")), P("blk", None))
    return jax.shard_map(
        on_device,
        mesh=mesh,
        in_specs=placed,
        out_specs=(P(("had", "blk"), None), P(), P()),
        check_vma=False,
    )
```

profile of v0, /device:TPU:0, one launch (start us, length us, event | category | flops | bytes accessed | tf_op | source)
XLA Modules:
  0.0 1226.9 jit_solution(7551053319992622696)
XLA Ops:
  7.9 1.8 negate_select_fusion
  9.7 2.6 fusion.96
  12.5 11.7 gather_fusion
  24.2 3.9 select_multiply_fusion
  28.4 145.2 %all-reduce.22.cloned.1.call-done = f32[2048,512]{1,0:T(8,128)} async-done(((f32[2048,512]{1,0:T(8,128)}), f32[2048,512]{1,0:T(8,128)}) %all-reduce.22.cloned.1.call-update) | async-done | bytes 4194320 | tf_op jit(solution)/shard_map/psum | solution.py:80
  173.6 10.5 fusion.185
  185.7 11.7 cholesky.286
  197.6 9.8 custom-call.59
  209.9 11.7 cholesky.305
  221.6 10.2 custom-call.60
  233.4 11.7 cholesky.326
  245.2 9.8 custom-call.61
  256.4 11.7 cholesky.343
  272.9 4.7 gather_fusion.1
  278.0 68.4 %reshape.325 = f32[256,2,256,2]{3,2,1,0:T(8,128)} reshape(f32[512,512]{1,0:T(8,128)S(1)} %select_select_fusion.1) | data formatting | bytes 2097152 | tf_op jit(solution)/shard_map/reshape | solution.py:34
  346.4 35.9 %reshape.326 = f32[128,4,128,4]{3,2,1,0:T(8,128)} reshape(f32[512,512]{1,0:T(8,128)S(1)} %select_select_fusion.1) | data formatting | bytes 2097152 | tf_op jit(solution)/shard_map/reshape | solution.py:34
  382.3 11.0 reshape.327
  393.3 4.9 reshape.328
  398.2 2.5 reshape.329
  400.7 1.7 reshape.330
  403.7 1.6 reshape.332
  406.7 107.3 %copy.213 = f32[256,2,256,2]{3,1,2,0:T(2,128)} copy(f32[256,2,256,2]{3,2,1,0:T(8,128)} %reshape.325) | data formatting | bytes 2097152 | tf_op jit(solution)/shard_map/reshape | solution.py:34
  514.0 2.5 gather_fusion.2
  517.3 38.0 %copy.215 = f32[128,4,128,4]{3,1,2,0:T(4,128)} copy(f32[128,4,128,4]{3,2,1,0:T(8,128)} %reshape.326) | data formatting | bytes 2097152 | tf_op jit(solution)/shard_map/reshape | solution.py:34
  555.4 1.9 gather_fusion.3
  559.5 20.5 %copy.217 = f32[64,8,64,8]{3,1,2,0:T(8,128)} copy(f32[64,8,64,8]{3,2,1,0:T(8,128)} %reshape.327) | data formatting | bytes 2097152 | tf_op jit(solution)/shard_map/reshape | solution.py:34
  580.0 6.4 gather_fusion.4
  587.8 14.2 %copy.219 = f32[32,16,32,16]{3,1,2,0:T(8,128)} copy(f32[32,16,32,16]{3,2,1,0:T(8,128)} %reshape.328) | data formatting | bytes 2097152 | tf_op jit(solution)/shard_map/reshape | solution.py:34
  602.0 4.0 gather_fusion.5
  606.8 5.4 copy.221
  612.3 2.8 gather_fusion.6
  615.8 3.3 copy.223
  619.2 2.2 gather_fusion.7
  629.1 2.9 convolution_convert_fusion.1
  633.3 2.3 fusion.186
  637.0 128.6 %all-reduce.24.cloned.1.call-done = f32[512,512]{0,1:T(8,128)} async-done(((f32[512,512]{0,1:T(8,128)}), f32[512,512]{0,1:T(8,128)}) %all-reduce.24.cloned.1.call-update) | async-done | bytes 1048592 | tf_op jit(solution)/shard_map/psum | solution.py:90
  765.7 1.4 broadcast_multiply_fusion
  767.7 11.7 cholesky.358
  779.6 10.0 custom-call.62
  790.2 11.7 cholesky.377
  802.0 9.8 custom-call.63
  812.5 11.7 cholesky.398
  824.2 10.3 custom-call.64
  835.1 11.7 cholesky.415
  852.3 4.5 gather_fusion.10
  857.2 68.4 %reshape.336 = f32[256,2,256,2]{3,2,1,0:T(8,128)} reshape(f32[512,512]{1,0:T(8,128)S(1)} %select_select_fusion) | data formatting | bytes 2097152 | tf_op jit(solution)/shard_map/reshape | solution.py:34
  925.6 35.9 %reshape.337 = f32[128,4,128,4]{3,2,1,0:T(8,128)} reshape(f32[512,512]{1,0:T(8,128)S(1)} %select_select_fusion) | data formatting | bytes 2097152 | tf_op jit(solution)/shard_map/reshape | solution.py:34
  961.5 11.0 reshape.338
  972.5 4.9 reshape.339
  977.4 2.6 reshape.340
  980.0 1.7 reshape.341
  983.1 1.7 reshape.343
  986.3 107.3 %copy.212 = f32[256,2,256,2]{3,1,2,0:T(2,128)} copy(f32[256,2,256,2]{3,2,1,0:T(8,128)} %reshape.336) | data formatting | bytes 2097152 | tf_op jit(solution)/shard_map/reshape | solution.py:34
  1093.6 2.5 gather_fusion.11
  1096.9 37.8 %copy.214 = f32[128,4,128,4]{3,1,2,0:T(4,128)} copy(f32[128,4,128,4]{3,2,1,0:T(8,128)} %reshape.337) | data formatting | bytes 2097152 | tf_op jit(solution)/shard_map/reshape | solution.py:34
  1134.7 1.9 gather_fusion.12
  1138.9 20.3 %copy.216 = f32[64,8,64,8]{3,1,2,0:T(8,128)} copy(f32[64,8,64,8]{3,2,1,0:T(8,128)} %reshape.338) | data formatting | bytes 2097152 | tf_op jit(solution)/shard_map/reshape | solution.py:34
  1159.2 6.4 gather_fusion.13
  1167.0 14.2 %copy.218 = f32[32,16,32,16]{3,1,2,0:T(8,128)} copy(f32[32,16,32,16]{3,2,1,0:T(8,128)} %reshape.339) | data formatting | bytes 2097152 | tf_op jit(solution)/shard_map/reshape | solution.py:34
  1181.2 4.0 gather_fusion.14
  1186.1 5.4 copy.220
  1191.5 2.8 gather_fusion.15
  1196.5 2.0 copy.222
  1215.4 4.2 convolution_convert_fusion
  (204 shorter events, 62.8 us)
Async XLA Ops:
  7.2 166.4 %all-reduce.22.cloned.1.call-start = ((), (), s32[]{:S(2)}) async-start(), calls=%async_computation | async-start | bytes 8388608 | tf_op jit(solution)/shard_map/psum | solution.py:80
  9.7 2.7 copy-start.22
  28.2 737.5 %all-reduce.24.cloned.1.call-start = ((), (), s32[]{:S(2)}) async-start(), calls=%async_computation.1 | async-start | bytes 2097152 | tf_op jit(solution)/shard_map/psum | solution.py:90
  28.2 527.1 %copy-start.4 = (s32[128]{0:T(128)}, s32[128]{0:T(128)S(1)}, u32[]{:S(2)}) copy-start(s32[128]{0:T(128)S(1)} %or_bitcast_fusion.6) | copy-start | bytes 1540
  28.3 551.8 %copy-start.6 = (s32[64]{0:T(128)}, s32[64]{0:T(128)S(1)}, u32[]{:S(2)}) copy-start(s32[64]{0:T(128)S(1)} %or_bitcast_fusion.5) | copy-start | bytes 772
  28.3 573.7 %copy-start.15 = (s32[32]{0:T(128)}, s32[32]{0:T(128)S(1)}, u32[]{:S(2)}) copy-start(s32[32]{0:T(128)S(1)} %or_bitcast_fusion.4) | copy-start | bytes 388
  28.3 583.9 %copy-start.17 = (s32[16]{0:T(128)}, s32[16]{0:T(128)S(1)}, u32[]{:S(2)}) copy-start(s32[16]{0:T(128)S(1)} %or_bitcast_fusion.3) | copy-start | bytes 196
  28.3 590.8 %copy-start.20 = (s32[8]{0:T(128)}, s32[8]{0:T(128)S(1)}, u32[]{:S(2)}) copy-start(s32[8]{0:T(128)S(1)} %or_bitcast_fusion.2) | copy-start | bytes 100
  28.4 595.0 %copy-start.23 = (s32[4]{0:T(128)}, s32[4]{0:T(128)S(1)}, u32[]{:S(2)}) copy-start(s32[4]{0:T(128)S(1)} %or_bitcast_fusion.1) | copy-start | bytes 52
  28.4 485.6 %copy-start.2 = (s32[256,1]{0,1:T(1,128)}, s32[256,1]{0,1:T(1,128)S(1)}, u32[]{:S(2)}) copy-start(s32[256,1]{0,1:T(1,128)S(1)} %shift-left_or_fusion.1) | copy-start | bytes 3076
  28.4 244.4 %copy-start = (s32[512,1]{0,1:T(1,128)}, s32[512,1]{0,1:T(1,128)S(1)}, u32[]{:S(2)}) copy-start(s32[512,1]{0,1:T(1,128)S(1)} %shift-left_or_fusion) | copy-start | bytes 6148
  184.7 1.0 copy-start.10
  632.0 1.3 copy-start.25
  765.7 1.8 copy-start.8
  767.7 84.6 %copy-start.1 = (s32[512,1]{0,1:T(1,128)S(1)}, s32[512,1]{0,1:T(1,128)}, u32[]{:S(2)}) copy-start(s32[512,1]{0,1:T(1,128)} %copy-done) | copy-start | bytes 6148
  986.3 107.3 %copy-start.3 = (s32[256,1]{0,1:T(1,128)S(1)}, s32[256,1]{0,1:T(1,128)}, u32[]{:S(2)}) copy-start(s32[256,1]{0,1:T(1,128)} %copy-done.2) | copy-start | bytes 3076
  1096.9 37.8 %copy-start.5 = (s32[128]{0:T(128)S(1)}, s32[128]{0:T(128)}, u32[]{:S(2)}) copy-start(s32[128]{0:T(128)} %copy-done.4) | copy-start | bytes 1540
  1138.9 20.3 %copy-start.7 = (s32[64]{0:T(128)S(1)}, s32[64]{0:T(128)}, u32[]{:S(2)}) copy-start(s32[64]{0:T(128)} %copy-done.6) | copy-start | bytes 772
  1167.0 14.2 %copy-start.16 = (s32[32]{0:T(128)S(1)}, s32[32]{0:T(128)}, u32[]{:S(2)}) copy-start(s32[32]{0:T(128)} %copy-done.15) | copy-start | bytes 388
  1186.0 5.4 copy-start.18
  1191.5 7.0 copy-start.21
  1195.1 0.7 copy-start.11
  1198.5 6.7 copy-start.24
  1202.4 0.7 copy-start.12
  1205.1 5.3 copy-start.9
  1209.1 0.7 copy-start.13
  1210.6 1.0 copy-start.14
  1210.6 1.7 copy-start.19
Sparse Core Ops, SparseCore 0:
  28.3 145.2 all-reduce.21
  635.7 129.9 all-reduce.23
where the time goes:
time: 1230 us
  local copies, waits for them, and re-layouts  708 us (58%)
  waiting for transfers between devices  274 us (22%)
  other arithmetic  175 us (14%)
  matrix products  49 us (4%)
  between operations  21 us (2%)
    reshape x32, local copies, waits for them, and re-layouts, lower_inverse(): tiles = lower.reshape(count, 2 * width, count, 2 * width)  635 us
    another operation x29, other arithmetic, upper_factor(): return jnp.linalg.cholesky(matrix).T  158 us
    psum x1, waiting for transfers between devices, on_device(): sketch = lax.psum(partial_sketch, ('had', 'blk'))  145 us
    psum x1, waiting for transfers between devices, on_device(): summed = lax.psum(partial_gram, ('had', 'blk'))  129 us
    gather x16, local copies, waits for them, and re-layouts, lower_inverse(): diag_tiles = jnp.moveaxis(jnp.diagonal(tiles, axis1=0, axis2=2), -1, 0)  40.2 us
  transfers between devices with their start and end apart: 2, of which 2 were waited for; matrix products, arithmetic and copies ran while one was open for 0% of the time, Pallas kernels for 0%

commit v1 on v0

--- a/solution.py
+++ b/solution.py
@@ -77,7 +77,8 @@
     parity = bit_parity(jnp.bitwise_and(owners, my_group))
     weights = (1 - 2 * parity).astype(jnp.float32) * factor
     partial_sketch = jnp.take(mixed, offsets, axis=0) * weights[:, None]
-    sketch = lax.psum(partial_sketch, ("had", "blk"))
+    parts = lax.all_gather(partial_sketch, ("had", "blk"), axis=0, tiled=False)
+    sketch = parts.sum(axis=0)
     sketch_gram = jnp.dot(
         sketch.T, sketch, precision=lax.Precision.HIGHEST, preferred_element_type=jnp.float32
     )

time: 1230 us -> 1810 us (1.47)
  waiting for transfers between devices: 274 us -> 805 us
  other arithmetic: 175 us -> 221 us
    all_gather x0 -> x1, waiting for transfers between devices: none -> 678 us  [on_device(): parts = lax.all_gather(partial_sketch, ('had', 'blk'), axis=0, tiled=False)]
    psum x1 -> x0, waiting for transfers between devices: 145 us -> none  [on_device(): sketch = lax.psum(partial_sketch, ('had', 'blk'))]
    reduce_sum x0 -> x1, other arithmetic: none -> 42.8 us  [on_device(): sketch = parts.sum(axis=0)]
where the time goes in v1:
time: 1810 us; the launch traced here: 1800 us
  waiting for transfers between devices  805 us (44%)
  local copies, waits for them, and re-layouts  708 us (39%)
  other arithmetic  221 us (12%)
  matrix products  49.2 us (3%)
  between operations  20.9 us (1%)
    all_gather x1, waiting for transfers between devices, on_device(): parts = lax.all_gather(partial_sketch, ('had', 'blk'), axis=0, tiled=False)  678 us
    reshape x32, local copies, waits for them, and re-layouts, lower_inverse(): tiles = lower.reshape(count, 2 * width, count, 2 * width)  635 us
    another operation x29, other arithmetic, upper_factor(): return jnp.linalg.cholesky(matrix).T  158 us
    psum x1, waiting for transfers between devices, on_device(): summed = lax.psum(partial_gram, ('had', 'blk'))  128 us
    reduce_sum x1, other arithmetic, on_device(): sketch = parts.sum(axis=0)  42.8 us
    gather x16, local copies, waits for them, and re-layouts, lower_inverse(): diag_tiles = jnp.moveaxis(jnp.diagonal(tiles, axis1=0, axis2=2), -1, 0)  40.3 us
  transfers between devices with their start and end apart: 2, of which 2 were waited for; matrix products, arithmetic and copies ran while one was open for 0% of the time, Pallas kernels for 0%

profile of v1, /device:TPU:0, one launch (start us, length us, event | category | flops | bytes accessed | tf_op | source)
XLA Modules:
  0.0 1804.3 jit_solution(6527619167056811034)
XLA Ops:
  7.9 1.8 negate_select_fusion
  9.7 2.7 fusion.97
  12.5 11.7 gather_fusion
  24.2 3.9 fusion
  31.5 677.6 %all-gather.2.cloned.1.call-done = f32[32,2048,512]{2,1,0:T(8,128)} async-done(((f32[1,2048,512]{2,1,0:T(8,128)}), f32[32,2048,512]{2,1,0:T(8,128)}) %all-gather.2.cloned.1.call-update) | async-done | bytes 134217744 | tf_op jit(solution)/shard_map/all_gather | solution.py:80
  709.1 42.8 %reduce_sum.9 = f32[2048,512]{1,0:T(8,128)} reduce(f32[32,2048,512]{2,1,0:T(8,128)} %all-gather.2.cloned.1.call-done, f32[]{:T(128)} %constant.290.clone.1), dimensions={0}, to_apply=%region_0.1 | reduce | flops 32505856 | bytes 138412032 | tf_op jit(solution)/shard_map/reduce_sum | solution.py:81
  751.8 10.7 fusion.186
  764.0 11.7 cholesky.286
  775.9 9.8 custom-call.59
  788.3 11.7 cholesky.305
  800.0 10.2 custom-call.60
  811.8 11.7 cholesky.326
  823.5 9.8 custom-call.61
  834.8 11.7 cholesky.343
  851.2 4.7 gather_fusion.1
  856.3 68.4 %reshape.370 = f32[256,2,256,2]{3,2,1,0:T(8,128)} reshape(f32[512,512]{1,0:T(8,128)S(1)} %select_select_fusion.1) | data formatting | bytes 2097152 | tf_op jit(solution)/shard_map/reshape | solution.py:34
  924.7 35.9 %reshape.371 = f32[128,4,128,4]{3,2,1,0:T(8,128)} reshape(f32[512,512]{1,0:T(8,128)S(1)} %select_select_fusion.1) | data formatting | bytes 2097152 | tf_op jit(solution)/shard_map/reshape | solution.py:34
  960.6 11.1 reshape.372
  971.7 4.9 reshape.373
  976.6 2.5 reshape.374
  979.0 1.7 reshape.375
  982.1 1.6 reshape.377
  985.1 107.3 %copy.213 = f32[256,2,256,2]{3,1,2,0:T(2,128)} copy(f32[256,2,256,2]{3,2,1,0:T(8,128)} %reshape.370) | data formatting | bytes 2097152 | tf_op jit(solution)/shard_map/reshape | solution.py:34
  1092.4 2.5 gather_fusion.2
  1095.8 38.0 %copy.215 = f32[128,4,128,4]{3,1,2,0:T(4,128)} copy(f32[128,4,128,4]{3,2,1,0:T(8,128)} %reshape.371) | data formatting | bytes 2097152 | tf_op jit(solution)/shard_map/reshape | solution.py:34
  1133.8 1.9 gather_fusion.3
  1138.0 20.5 %copy.217 = f32[64,8,64,8]{3,1,2,0:T(8,128)} copy(f32[64,8,64,8]{3,2,1,0:T(8,128)} %reshape.372) | data formatting | bytes 2097152 | tf_op jit(solution)/shard_map/reshape | solution.py:34
  1158.5 6.4 gather_fusion.4
  1166.2 14.2 copy.219
  1180.4 4.0 gather_fusion.5
  1185.3 5.4 copy.221
  1190.7 2.8 gather_fusion.6
  1194.3 3.3 copy.223
  1197.7 2.2 gather_fusion.7
  1207.6 2.9 convolution_convert_fusion.1
  1211.8 2.3 fusion.187
  1215.6 127.5 %all-reduce.21.cloned.1.call-done = f32[512,512]{0,1:T(8,128)} async-done(((f32[512,512]{0,1:T(8,128)}), f32[512,512]{0,1:T(8,128)}) %all-reduce.21.cloned.1.call-update) | async-done | bytes 1048592 | tf_op jit(solution)/shard_map/psum | solution.py:91
  1345.1 11.7 cholesky.358
  1357.0 10.0 custom-call.62
  1367.7 11.7 cholesky.377
  1379.4 9.8 custom-call.63
  1389.9 11.7 cholesky.398
  1401.6 10.2 custom-call.64
  1412.5 11.7 cholesky.415
  1429.5 4.5 gather_fusion.10
  1434.5 68.4 %reshape.381 = f32[256,2,256,2]{3,2,1,0:T(8,128)} reshape(f32[512,512]{1,0:T(8,128)S(1)} %select_select_fusion) | data formatting | bytes 2097152 | tf_op jit(solution)/shard_map/reshape | solution.py:34
  1502.9 35.9 %reshape.382 = f32[128,4,128,4]{3,2,1,0:T(8,128)} reshape(f32[512,512]{1,0:T(8,128)S(1)} %select_select_fusion) | data formatting | bytes 2097152 | tf_op jit(solution)/shard_map/reshape | solution.py:34
  1538.8 11.1 reshape.383
  1549.9 4.9 reshape.384
  1554.8 2.6 reshape.385
  1557.4 1.7 reshape.386
  1560.4 1.7 reshape.388
  1563.6 107.3 %copy.212 = f32[256,2,256,2]{3,1,2,0:T(2,128)} copy(f32[256,2,256,2]{3,2,1,0:T(8,128)} %reshape.381) | data formatting | bytes 2097152 | tf_op jit(solution)/shard_map/reshape | solution.py:34
  1671.0 2.5 gather_fusion.11
  1674.3 37.8 %copy.214 = f32[128,4,128,4]{3,1,2,0:T(4,128)} copy(f32[128,4,128,4]{3,2,1,0:T(8,128)} %reshape.382) | data formatting | bytes 2097152 | tf_op jit(solution)/shard_map/reshape | solution.py:34
  1712.1 1.9 gather_fusion.12
  1716.3 20.3 %copy.216 = f32[64,8,64,8]{3,1,2,0:T(8,128)} copy(f32[64,8,64,8]{3,2,1,0:T(8,128)} %reshape.383) | data formatting | bytes 2097152 | tf_op jit(solution)/shard_map/reshape | solution.py:34
  1736.6 6.4 gather_fusion.13
  1744.4 14.2 copy.218
  1758.6 4.0 gather_fusion.14
  1763.4 5.4 copy.220
  1768.9 2.8 gather_fusion.15
  1773.9 2.0 copy.222
  1792.8 4.2 convolution_convert_fusion
  (207 shorter events, 67.4 us)
Async XLA Ops:
  7.2 701.9 %all-gather.2.cloned.1.call-start = ((), (), s32[]{:S(2)}) async-start(), calls=%async_computation | async-start | bytes 138412032 | tf_op jit(solution)/shard_map/all_gather | solution.py:80
  9.7 2.7 copy-start.22
  28.1 1315.0 %all-reduce.21.cloned.1.call-start = ((), (), s32[]{:S(2)}) async-start(), calls=%async_computation.1 | async-start | bytes 2097152 | tf_op jit(solution)/shard_map/psum | solution.py:91
  28.2 1105.6 %copy-start.4 = (s32[128]{0:T(128)}, s32[128]{0:T(128)S(1)}, u32[]{:S(2)}) copy-start(s32[128]{0:T(128)S(1)} %or_bitcast_fusion.6) | copy-start | bytes 1540
  31.5 1060.9 %copy-start.2 = (s32[256,1]{0,1:T(1,128)}, s32[256,1]{0,1:T(1,128)S(1)}, u32[]{:S(2)}) copy-start(s32[256,1]{0,1:T(1,128)S(1)} %shift-left_or_fusion.1) | copy-start | bytes 3076
  31.5 819.7 %copy-start = (s32[512,1]{0,1:T(1,128)}, s32[512,1]{0,1:T(1,128)S(1)}, u32[]{:S(2)}) copy-start(s32[512,1]{0,1:T(1,128)S(1)} %shift-left_or_fusion) | copy-start | bytes 6148
  763.1 1.0 copy-start.10
  1138.0 20.5 %copy-start.6 = (s32[64]{0:T(128)S(1)}, s32[64]{0:T(128)}, u32[]{:S(2)}) copy-start(s32[64]{0:T(128)} %or_bitcast_fusion.5) | copy-start | bytes 772
  1166.2 14.2 copy-start.15
  1185.3 5.5 copy-start.17
  1190.7 6.9 copy-start.20
  1197.7 4.2 copy-start.23
  1201.8 2.6 copy-start.25
  1210.5 1.4 copy-start.26
  1343.1 1.8 copy-start.8
  1345.1 84.5 %copy-start.1 = (s32[512,1]{0,1:T(1,128)S(1)}, s32[512,1]{0,1:T(1,128)}, u32[]{:S(2)}) copy-start(s32[512,1]{0,1:T(1,128)} %copy-done) | copy-start | bytes 6148
  1563.6 107.3 %copy-start.3 = (s32[256,1]{0,1:T(1,128)S(1)}, s32[256,1]{0,1:T(1,128)}, u32[]{:S(2)}) copy-start(s32[256,1]{0,1:T(1,128)} %copy-done.2) | copy-start | bytes 3076
  1674.3 37.8 %copy-start.5 = (s32[128]{0:T(128)S(1)}, s32[128]{0:T(128)}, u32[]{:S(2)}) copy-start(s32[128]{0:T(128)} %copy-done.4) | copy-start | bytes 1540
  1716.3 20.3 %copy-start.7 = (s32[64]{0:T(128)S(1)}, s32[64]{0:T(128)}, u32[]{:S(2)}) copy-start(s32[64]{0:T(128)} %or_bitcast_fusion.5) | copy-start | bytes 772
  1744.4 14.2 copy-start.16
  1763.4 5.5 copy-start.18
  1768.9 7.0 copy-start.21
  1772.5 0.7 copy-start.11
  1775.9 6.7 copy-start.24
  1779.8 0.7 copy-start.12
  1782.6 5.3 copy-start.9
  1786.5 0.7 copy-start.13
  1788.0 1.0 copy-start.14
  1788.0 1.7 copy-start.19
Sparse Core Ops, SparseCore 0:
  28.2 680.7 all-gather.1
  1214.2 128.7 all-reduce.20
